TPU v7x, 128 devices: a whole 4x4x4 slice. The times are simulated.
128 devices in a mesh: dp: 8 (over z, core), tensor: 16 (over y, x).
Axes of the slice: x: 4, y: 4, z: 4, core: 2. Of those that a mesh axis runs over, the one named last changes fastest.
Arguments:
- residues: bfloat16 [4096, 1024], P('dp'), may hold values from -40 to 40
- block_protein: int32 [32], P('dp'), may hold values from 0 to 31, as said below
- protein_length: int32 [32], replicated, may hold values from 0 to 256, as said below
- decoder_group: int32 [32], replicated, may hold values from 0 to 7, as said below
- enc_gain: float32 [1024], replicated, may hold values from 0.1 to 1.9
- enc_query: bfloat16 [1024, 16384], P(None, 'tensor'), may hold values from -2 to 2
- enc_key: bfloat16 [1024, 16384], P(None, 'tensor'), may hold values from -2 to 2
- enc_value: bfloat16 [1024, 16384], P(None, 'tensor'), may hold values from -0.1875 to 0.1875
- enc_out: bfloat16 [16384, 1024], P('tensor'), may hold values from -0.1875 to 0.1875
- decoder_states: bfloat16 [3072, 1024], P('dp'), may hold values from -40 to 40
- query_protein: int32 [3072], P('dp'), may hold values from 0 to 31, as said below
- dec_gain: float32 [1024], replicated, may hold values from 0.1 to 1.9
- final_gain: float32 [1024], replicated, may hold values from 0.1 to 1.9
- cross_query: bfloat16 [1024, 16384], P(None, 'tensor'), may hold values from -2 to 2
- cross_key: bfloat16 [1024, 16384], P(None, 'tensor'), may hold values from -2 to 2
- cross_value: bfloat16 [1024, 16384], P(None, 'tensor'), may hold values from -0.1875 to 0.1875
- cross_out: bfloat16 [16384, 1024], P('tensor'), may hold values from -0.1875 to 0.1875
Outputs:
- encoded: bfloat16 [4096, 1024], P('dp', 'tensor')
- decoded: bfloat16 [3072, 1024], P(('dp', 'tensor'))
Inputs may be any that keep to these rules, and one draw needn't show every extreme that they name: `block_protein`: block b of dp group d names a protein id from d * 4 to (d + 1) * 4 - 1; the blocks of one protein are consecutive and the ids rise along a group's blocks. `protein_length`: A protein of n blocks has a length from (n - 1) * 128 + 1 to n * 128; an id that no block names has length 0; no protein spans more than 2 blocks. `decoder_group`: at most 2 blocks of one dp group belong to proteins of one decoder group, and in every draw some decoder group gets exactly 2 blocks from every dp group; every decoder group owns a protein of positive length. `query_protein`: query row i names a protein of positive length whose decoder group is i // 384.
All inputs are finite; a program needn't handle non-finite values.
Results may differ from a plain program's by a relative error of at most 0.017.
Values may be sent and summed in bfloat16 or wider, within the bound.
No kernel may reach another device: no remote copies, remote signals or barrier semaphores. Data moves between devices by JAX's collectives and lax.ppermute only.
A program may use at most 128 MiB of HBM per device.

v0:
```python
import jax
import jax.numpy as jnp
from jax import lax
from jax.sharding import PartitionSpec as P

HEAD_DIM = 128
BLOCK = 128
EPSILON = 1e-06
MASKED = -1000000000.0


def split_up(x, dim, size):
    before, after = (x.shape[:dim], x.shape[dim + 1 :])
    return jnp.moveaxis(x.reshape(*before, size, -1, *after), dim, 0)


def sent_and_summed(x, axis, dim):
    blocks = split_up(x, dim, lax.axis_size(axis))
    arrived = lax.all_to_all(blocks, axis, split_axis=0, concat_axis=0, tiled=True)
    return arrived.sum(axis=0)


def summed_on_arrival(x, axis, dim):
    blocks = split_up(x, dim, lax.axis_size(axis))
    arrived = lax.all_to_all(blocks, axis, split_axis=0, concat_axis=0, tiled=True)
    return arrived.astype(jnp.float32).sum(axis=0)


def row_scale(matrix):
    values = matrix.astype(jnp.float32)
    return lax.rsqrt(jnp.mean(values * values, axis=1, keepdims=True) + EPSILON)


def table_lookup(indices, table):
    match = indices[:, None] == jnp.arange(table.shape[0], dtype=jnp.int32)[None, :]
    return jnp.sum(jnp.where(match, table[None, :], 0), axis=1)


def attend(queries, keys, values, allowed):
    count = queries.shape[0]
    heads = queries.shape[1] // HEAD_DIM
    query_heads = queries.reshape(count, heads, HEAD_DIM)
    key_heads = keys.reshape(keys.shape[0], heads, HEAD_DIM)
    value_heads = values.reshape(values.shape[0], heads, HEAD_DIM)
    scores = jnp.einsum(
        "qhd,khd->hqk", query_heads, key_heads, preferred_element_type=jnp.float32
    ) * HEAD_DIM ** (-0.5)
    scores = jnp.where(allowed[None], scores, MASKED)
    top = jnp.max(scores, axis=2, keepdims=True)
    expo = jnp.exp(scores - top)
    total = jnp.sum(expo, axis=2)
    weights = expo.astype(jnp.bfloat16)
    context = jnp.einsum("hqk,khd->qhd", weights, value_heads, preferred_element_type=jnp.float32)
    context = context / jnp.transpose(total)[:, :, None]
    return context.reshape(count, heads * HEAD_DIM).astype(jnp.bfloat16)


def body(
    residues,
    block_protein,
    protein_length,
    decoder_group,
    enc_gain,
    enc_query,
    enc_key,
    enc_value,
    enc_out,
    decoder_states,
    query_protein,
    dec_gain,
    final_gain,
    cross_query,
    cross_key,
    cross_value,
    cross_out,
):
    groups = lax.axis_size("dp")
    tensor_count = lax.axis_size("tensor")
    tensor_index = lax.axis_index("tensor")
    tok_rows = residues.shape[0]
    width = residues.shape[1]
    blocks = block_protein.shape[0]
    slots = blocks // 2
    order = jnp.arange(blocks, dtype=jnp.int32)
    same = block_protein[:, None] == block_protein[None, :]
    offset = jnp.sum(same & (order[None, :] < order[:, None]), axis=1)
    live = jnp.clip(table_lookup(block_protein, protein_length) - offset * BLOCK, 0, BLOCK)
    dest = table_lookup(block_protein, decoder_group)
    position = jnp.arange(BLOCK, dtype=jnp.int32)
    token_protein = jnp.broadcast_to(block_protein[:, None], (blocks, BLOCK)).reshape(tok_rows)
    token_valid = (position[None, :] < live[:, None]).reshape(tok_rows)
    normed = (residues.astype(jnp.float32) * row_scale(residues) * enc_gain[None, :]).astype(
        jnp.bfloat16
    )
    enc_queries = jnp.dot(normed, enc_query, preferred_element_type=jnp.float32).astype(
        jnp.bfloat16
    )
    enc_keys = jnp.dot(normed, enc_key, preferred_element_type=jnp.float32).astype(jnp.bfloat16)
    enc_values = jnp.dot(normed, enc_value, preferred_element_type=jnp.float32).astype(jnp.bfloat16)
    row_block = min(tok_rows, 512)
    block_count = tok_rows // row_block

    def encode_block(item):
        block_queries, block_owner = item
        permit = (block_owner[:, None] == token_protein[None, :]) & token_valid[None, :]
        return attend(block_queries, enc_keys, enc_values, permit)

    context = lax.map(
        encode_block,
        (
            enc_queries.reshape(block_count, row_block, -1),
            token_protein.reshape(block_count, row_block),
        ),
    )
    context = context.reshape(tok_rows, -1)
    partial_value = jnp.dot(context, enc_out, preferred_element_type=jnp.float32)
    slice_width = width // tensor_count
    column_start = tensor_index * slice_width
    same_dest = dest[:, None] == dest[None, :]
    rank = jnp.sum(same_dest & (order[None, :] < order[:, None]), axis=1)
    place = dest * slots + rank
    target = jnp.arange(groups * slots, dtype=jnp.int32)
    chosen = target[:, None] == place[None, :]
    occupied = jnp.any(chosen, axis=1)
    send_ids = jnp.where(
        occupied, jnp.sum(jnp.where(chosen, block_protein[None, :], 0), axis=1), -1
    )
    send_live = jnp.sum(jnp.where(chosen, live[None, :], 0), axis=1)
    send_meta = jnp.stack([send_ids, send_live], axis=-1).reshape(groups, slots, 2)
    shares = sent_and_summed(partial_value, "tensor", 1)
    own_columns = lax.dynamic_slice_in_dim(residues, column_start, slice_width, 1)
    encoded = (own_columns.astype(jnp.float32) + shares).astype(jnp.bfloat16)
    features = encoded.shape[1]
    stacked = encoded.reshape(blocks, BLOCK * features)
    placed = jnp.dot(
        chosen.astype(jnp.bfloat16), stacked, preferred_element_type=jnp.float32
    ).astype(jnp.bfloat16)
    slice_grid = lax.all_to_all(
        placed.reshape(groups, slots, BLOCK, features),
        "dp",
        split_axis=0,
        concat_axis=0,
        tiled=True,
    )
    meta = lax.all_to_all(send_meta, "dp", split_axis=0, concat_axis=0, tiled=True)
    flat = slice_grid.reshape(-1, slice_width)
    inner = cross_key.shape[1]
    values32 = lax.all_gather(flat, "tensor", axis=1, tiled=True).astype(jnp.float32)
    scaled = (values32 * final_gain[None, :]).astype(jnp.bfloat16)
    key_sum = jnp.dot(scaled, cross_key, preferred_element_type=jnp.float32)
    value_sum = jnp.dot(scaled, cross_value, preferred_element_type=jnp.float32)
    squares = jnp.sum(values32 * values32, axis=1, keepdims=True)
    key_sum, value_sum, squares = (key_sum, value_sum, squares)
    key_scale = lax.rsqrt(squares / width + EPSILON)
    grid_shape = (groups, slots, BLOCK, inner)
    key_grid = (key_sum * key_scale).astype(jnp.bfloat16).reshape(grid_shape)
    value_grid = (value_sum * key_scale).astype(jnp.bfloat16).reshape(grid_shape)
    key_ids = meta[:, :, 0]
    key_live = meta[:, :, 1]
    key_valid = position[None, None, :] < key_live[:, :, None]
    query_rows = decoder_states.shape[0]
    dec_normed = (
        decoder_states.astype(jnp.float32) * row_scale(decoder_states) * dec_gain[None, :]
    ).astype(jnp.bfloat16)
    cross_queries = jnp.dot(dec_normed, cross_query, preferred_element_type=jnp.float32).astype(
        jnp.bfloat16
    )
    allowed = (query_protein[:, None, None, None] == key_ids[None, :, :, None]) & key_valid[None]
    slot_total = groups * slots
    inner_width = key_grid.shape[3]
    cross_context = attend(
        cross_queries,
        key_grid.reshape(slot_total * BLOCK, inner_width),
        value_grid.reshape(slot_total * BLOCK, inner_width),
        allowed.reshape(query_rows, slot_total * BLOCK),
    )
    share_rows = query_rows // tensor_count
    mixed = summed_on_arrival(
        jnp.dot(cross_context, cross_out, preferred_element_type=jnp.float32).astype(jnp.bfloat16),
        "tensor",
        0,
    )
    own_rows = lax.dynamic_slice_in_dim(decoder_states, tensor_index * share_rows, share_rows, 0)
    decoded = (own_rows.astype(jnp.float32) + mixed).astype(jnp.bfloat16)
    return (encoded, decoded)


def solution(mesh):
    in_specs = (
        P("dp", None),
        P("dp"),
        P(),
        P(),
        P(),
        P(None, "tensor"),
        P(None, "tensor"),
        P(None, "tensor"),
        P("tensor", None),
        P("dp", None),
        P("dp"),
        P(),
        P(),
        P(None, "tensor"),
        P(None, "tensor"),
        P(None, "tensor"),
        P("tensor", None),
    )
    out_specs = (P("dp", "tensor"), P(("dp", "tensor"), None))
    return jax.shard_map(body, mesh=mesh, in_specs=in_specs, out_specs=out_specs, check_vma=False)
```

profile of v0, /device:TPU:0, one launch (start us, length us, event | category | flops | bytes accessed | tf_op | source)
XLA Modules:
  0.0 220.1 jit_solution(1068523723538875895)
XLA Ops:
  7.2 1.0 convert_reduce_fusion.2
  8.9 0.9 select_reduce_fusion.2
  10.1 1.5 fusion.17
  11.6 4.4 %fusion.31 = bf16[64,8,8,128]{3,2,1,0:T(8,128)(2,1)} fusion(bf16[1024,1024]{1,0:T(8,128)(2,1)} %param.22, bf16[512,1024]{1,0:T(8,128)(2,1)} %param.17, f32[1024]{0:T(1024)} %param.21, f32[512]{0:T(512)S(1)} %add_rsqrt_fusion.2), kind=kOutput, calls=%fused_computation.46 | convolution fusion | flops 1076363264 | bytes 4200448 | tf_op jit(solution)/shard_map/dot_general | solution.py:95
  16.0 2.3 %fusion.32 = bf16[64,8,8,128]{3,2,1,0:T(8,128)(2,1)} fusion(bf16[1024,1024]{1,0:T(8,128)(2,1)S(1)} %copy-done.11, bf16[512,1024]{1,0:T(8,128)(2,1)S(1)} %copy-done.6, f32[1024]{0:T(1024)S(1)} %copy-done.14, f32[512]{0:T(512)S(1)} %add_rsqrt_fusion.2), kind=kOutput, calls=%fused_computation.47 | convolution fusion | flops 1076363264 | bytes 4200448 | tf_op jit(solution)/shard_map/dot_general | solution.py:98
  18.3 2.3 %convolution_convert_fusion.3 = bf16[512,1024]{1,0:T(8,128)(2,1)} fusion(bf16[1024,1024]{1,0:T(8,128)(2,1)S(1)} %copy-done.12, bf16[512,1024]{1,0:T(8,128)(2,1)S(1)} %copy-done.6, f32[1024]{0:T(1024)S(1)} %copy-done.14, f32[512]{0:T(512)S(1)} %add_rsqrt_fusion.2), kind=kOutput, calls=%fused_computation.43 | convolution fusion | flops 1076363264 | bytes 4200448 | tf_op jit(solution)/shard_map/dot_general | solution.py:99
  20.6 2.3 %copy.107 = bf16[512,1024]{0,1:T(8,128)(2,1)} copy(bf16[512,1024]{1,0:T(8,128)(2,1)} %convolution_convert_fusion.3) | data formatting | bytes 2097152 | tf_op jit(solution)/shard_map/while/body/eval_jaxpr/reshape | solution.py:44
  22.9 4.0 %copy.91 = bf16[1024,1024]{0,1:T(8,128)(2,1)} copy(bf16[1024,1024]{1,0:T(8,128)(2,1)} %param.25) | data formatting | bytes 4194304 | tf_op args[8]
  27.1 3.2 %fusion.8 = (f32[8,512]{1,0:T(8,128)S(1)}, f32[8,512,512]{1,2,0:T(8,128)S(1)}) fusion(pred[512,512]{0,1:T(8,128)(4,1)S(1)} %compare_and_fusion, bf16[64,8,8,128]{3,2,1,0:T(8,128)(2,1)} %fusion.32, bf16[64,8,8,128]{3,2,1,0:T(8,128)(2,1)} %fusion.31), kind=kOutput, calls=%fused_computation.16 | convolution fusion | flops 543158272 | bytes 10764288 | tf_op jit(solution)/shard_map/while/body/eval_jaxpr/qhd,khd->hqk/dot_general | solution.py:45
  30.3 1.7 fusion.9
  32.1 2.6 %fusion.20 = bf16[512,8,128]{0,2,1:T(8,128)(2,1)S(1)} fusion(bf16[512,8,128]{0,2,1:T(8,128)(2,1)S(1)} %bitcast.70, f32[8,512,512]{1,2,0:T(8,128)S(1)} %get-tuple-element.33, f32[8,512]{1,0:T(8,128)S(1)} %get-tuple-element.32, pred[512,512]{0,1:T(8,128)(4,1)S(1)} %compare_and_fusion, f32[512,8]{0,1:T(8,128)S(1)} %bitcast.72), kind=kOutput, calls=%fused_computation.31 | convolution fusion | flops 546308096 | bytes 10780672 | tf_op jit(solution)/shard_map/while/body/eval_jaxpr/hqk,khd->qhd/dot_general | solution.py:53
  34.7 2.5 %convolution_bitcast_fusion = f32[16,512,64]{1,2,0:T(8,128)} fusion(bf16[512,1024,1]{0,1,2:T(8,128)(2,1)S(1)} %bitcast.77, bf16[16,64,1024]{2,1,0:T(8,128)(2,1)S(1)} %bitcast.69), kind=kOutput, calls=%fused_computation.34 | convolution fusion | flops 1073741824 | bytes 5242880 | tf_op jit(solution)/shard_map/dot_general | solution.py:116
  37.2 7.2 %all-to-all-start = ((f32[16,512,64]{1,2,0:T(8,128)}), f32[16,512,64]{1,2,0:T(8,128)}, u32[]{:S(2)}, u32[]{:S(2)}) async-start(f32[16,512,64]{1,2,0:T(8,128)} %convolution_bitcast_fusion), calls=%async_computation | async-start | bytes 4194304 | tf_op jit(solution)/shard_map/all_to_all | solution.py:19
  44.7 31.5 %all-to-all-done = f32[16,512,64]{1,2,0:T(8,128)} async-done(((f32[16,512,64]{1,2,0:T(8,128)}), f32[16,512,64]{1,2,0:T(8,128)}, u32[]{:S(2)}, u32[]{:S(2)}) %all-to-all-start) | async-done | bytes 2097184 | tf_op jit(solution)/shard_map/all_to_all | solution.py:19
  76.2 1.8 reduce_sum.122
  79.4 12.7 %all_to_all.20 = bf16[8,2,128,64]{2,3,1,0:T(8,128)(2,1)S(1)} all-to-all(bf16[8,2,128,64]{2,3,1,0:T(8,128)(2,1)S(1)} %copy.94), channel_id=1, replica_groups=mesh['dp'=8,'tensor'=16] {'dp'}, dimensions={0} | all-to-all | bytes 524288 | tf_op jit(solution)/shard_map/all_to_all | solution.py:138
  94.3 3.5 %all-to-all-start.2 = ((s32[8,2,2]{1,2,0:T(2,128)}), s32[8,2,2]{1,2,0:T(2,128)S(1)}, u32[]{:S(2)}, u32[]{:S(2)}) async-start(s32[8,2,2]{1,2,0:T(2,128)} %copy.96), calls=%async_computation.2 | async-start | bytes 16384 | tf_op jit(solution)/shard_map/all_to_all | solution.py:145
  97.8 1.4 fusion.25
  99.2 3.9 %fusion.33 = bf16[48,8,8,128]{3,2,1,0:T(8,128)(2,1)} fusion(bf16[1024,1024]{1,0:T(8,128)(2,1)} %param.30, bf16[384,1024]{1,0:T(8,128)(2,1)} %param.26, f32[1024]{0:T(1024)S(1)} %copy-done.15, f32[384]{0:T(512)S(1)} %add_rsqrt_fusion.1), kind=kOutput, calls=%fused_computation.48 | convolution fusion | flops 807272448 | bytes 3675648 | tf_op jit(solution)/shard_map/dot_general | solution.py:165
  103.3 1.3 bitcast_and_fusion
  104.6 2.2 copy.101
  106.8 33.9 %all-gather.2.cloned.1.call-done = bf16[2048,1024]{0,1:T(8,128)(2,1)} async-done(((bf16[2048,64]{0,1:T(8,128)(2,1)}), bf16[2048,1024]{0,1:T(8,128)(2,1)}) %all-gather.2.cloned.1.call-update) | async-done | bytes 4194320 | tf_op jit(solution)/shard_map/all_gather | solution.py:148
  140.7 3.2 %fusion.7 = f32[2048]{0:T(1024)S(1)} fusion(bf16[2048,1024]{0,1:T(8,128)(2,1)} %all-gather.2.cloned.1.call-done), kind=kLoop, calls=%fused_computation.11 | loop fusion | flops 6289408 | bytes 4202496 | tf_op jit(solution)/shard_map/reduce_sum | solution.py:152
  144.1 5.6 %multiply_convert_fusion = bf16[2048,1024]{0,1:T(8,128)(2,1)S(1)} fusion(bf16[1024,1024]{1,0:T(8,128)(2,1)S(1)} %copy-done, f32[2048]{0:T(1024)S(1)} %add_rsqrt_fusion, bf16[2048,1024]{0,1:T(8,128)(2,1)S(1)} %copy-done.2, f32[1024]{0:T(1024)S(1)} %copy-done.16), kind=kOutput, calls=%fused_computation.12 | convolution fusion | flops 4305453056 | bytes 10498048 | tf_op jit(solution)/shard_map/dot_general | solution.py:150
  149.8 10.9 %fusion = (f32[8,384]{1,0:T(8,128)S(1)}, f32[8,384,2048]{2,1,0:T(8,128)}) fusion(pred[384,2048]{1,0:T(8,128)(4,1)S(1)} %copy.101, bf16[2048,8,128]{0,2,1:T(8,128)(2,1)S(1)} %bitcast.68, bf16[48,8,8,128]{3,2,1,0:T(8,128)(2,1)S(1)} %copy-done.5), kind=kOutput, calls=%fused_computation.2 | convolution fusion | flops 1629484032 | bytes 30945280 | tf_op jit(solution)/shard_map/qhd,khd->hqk/dot_general | solution.py:45
  160.7 11.7 %fusion.1 = f32[8,384]{1,0:T(8,128)S(1)} fusion(f32[8,384,2048]{2,1,0:T(8,128)} %get-tuple-element.35, f32[8,384]{1,0:T(8,128)S(1)} %get-tuple-element.34, pred[384,2048]{1,0:T(8,128)(4,1)S(1)} %copy.101), kind=kLoop, calls=%fused_computation.3 | loop fusion | flops 25162752 | bytes 25976832 | tf_op jit(solution)/shard_map/reduce_sum | solution.py:51
  172.4 5.6 %multiply_convert_fusion.1 = bf16[2048,1024]{0,1:T(8,128)(2,1)S(1)} fusion(bf16[1024,1024]{1,0:T(8,128)(2,1)S(1)} %copy-done.13, f32[2048]{0:T(1024)S(1)} %add_rsqrt_fusion, bf16[2048,1024]{0,1:T(8,128)(2,1)S(1)} %copy-done.2, f32[1024]{0:T(1024)S(1)} %copy-done.16), kind=kOutput, calls=%fused_computation.13 | convolution fusion | flops 4305453056 | bytes 10498048 | tf_op jit(solution)/shard_map/dot_general | solution.py:151
  178.1 12.2 %fusion.28 = bf16[384,8,128]{0,2,1:T(8,128)(2,1)S(1)} fusion(bf16[2048,8,128]{0,2,1:T(8,128)(2,1)S(1)} %bitcast.76, f32[8,384,2048]{2,1,0:T(8,128)} %get-tuple-element.35, f32[8,384]{1,0:T(8,128)S(1)} %get-tuple-element.34, pred[384,2048]{1,0:T(8,128)(4,1)S(1)} %copy.101, f32[384,8]{0,1:T(8,128)S(1)} %bitcast.75), kind=kOutput, calls=%fused_computation.39 | convolution fusion | flops 1636564992 | bytes 30957568 | tf_op jit(solution)/shard_map/hqk,khd->qhd/dot_general | solution.py:53
  190.3 1.9 convolution_convert_fusion.4
  192.1 5.3 %all-to-all-start.3 = ((bf16[16,24,1024]{2,1,0:T(8,128)(2,1)}), bf16[16,24,1024]{2,1,0:T(8,128)(2,1)S(1)}, u32[]{:S(2)}, u32[]{:S(2)}) async-start(bf16[16,24,1024]{2,1,0:T(8,128)(2,1)} %bitcast.18), calls=%async_computation.3 | async-start | bytes 1572864 | tf_op jit(solution)/shard_map/all_to_all | solution.py:25
  197.4 14.3 %all-to-all-done.3 = bf16[16,24,1024]{2,1,0:T(8,128)(2,1)S(1)} async-done(((bf16[16,24,1024]{2,1,0:T(8,128)(2,1)}), bf16[16,24,1024]{2,1,0:T(8,128)(2,1)S(1)}, u32[]{:S(2)}, u32[]{:S(2)}) %all-to-all-start.3) | async-done | bytes 786464 | tf_op jit(solution)/shard_map/all_to_all | solution.py:25
  211.8 1.4 add_convert_fusion.1
  (67 shorter events, 5.6 us)
Async XLA Ops:
  7.2 136.7 %copy-start = (bf16[1024,1024]{1,0:T(8,128)(2,1)S(1)}, bf16[1024,1024]{1,0:T(8,128)(2,1)}, u32[]{:S(2)}) copy-start(bf16[1024,1024]{1,0:T(8,128)(2,1)} %param.31) | copy-start | bytes 6291460
  11.6 4.4 %copy-start.6 = (bf16[512,1024]{1,0:T(8,128)(2,1)S(1)}, bf16[512,1024]{1,0:T(8,128)(2,1)}, u32[]{:S(2)}) copy-start(bf16[512,1024]{1,0:T(8,128)(2,1)} %param.17) | copy-start | bytes 3145732
  11.6 4.4 %copy-start.11 = (bf16[1024,1024]{1,0:T(8,128)(2,1)S(1)}, bf16[1024,1024]{1,0:T(8,128)(2,1)}, u32[]{:S(2)}) copy-start(bf16[1024,1024]{1,0:T(8,128)(2,1)} %param.23) | copy-start | bytes 6291460
  11.6 4.4 %copy-start.14 = (f32[1024]{0:T(1024)S(1)}, f32[1024]{0:T(1024)}, u32[]{:S(2)}) copy-start(f32[1024]{0:T(1024)} %param.21) | copy-start | bytes 12292
  16.0 2.3 %copy-start.12 = (bf16[1024,1024]{1,0:T(8,128)(2,1)S(1)}, bf16[1024,1024]{1,0:T(8,128)(2,1)}, u32[]{:S(2)}) copy-start(bf16[1024,1024]{1,0:T(8,128)(2,1)} %param.24) | copy-start | bytes 6291460
  30.3 1.8 copy-start.7
  32.1 2.6 %copy-start.4 = (bf16[1024,1024]{0,1:T(8,128)(2,1)S(1)}, bf16[1024,1024]{0,1:T(8,128)(2,1)}, u32[]{:S(2)}) copy-start(bf16[1024,1024]{0,1:T(8,128)(2,1)} %copy.91) | copy-start | bytes 6291460
  37.2 39.0 %all-to-all-start = ((f32[16,512,64]{1,2,0:T(8,128)}), f32[16,512,64]{1,2,0:T(8,128)}, u32[]{:S(2)}, u32[]{:S(2)}) async-start(f32[16,512,64]{1,2,0:T(8,128)} %convolution_bitcast_fusion), calls=%async_computation | async-start | bytes 4194304 | tf_op jit(solution)/shard_map/all_to_all | solution.py:19
  44.4 49.0 %copy-start.9 = (s32[4]{0:T(128)S(1)}, s32[4]{0:T(128)}, u32[]{:S(2)}) copy-start(s32[4]{0:T(128)} %param.18) | copy-start | bytes 52
  44.4 54.8 %copy-start.15 = (f32[1024]{0:T(1024)S(1)}, f32[1024]{0:T(1024)}, u32[]{:S(2)}) copy-start(f32[1024]{0:T(1024)} %param.28) | copy-start | bytes 12292
  44.4 96.2 %all-gather.2.cloned.1.call-start = ((), (), s32[]{:S(2)}) async-start(), calls=%async_computation.4 | async-start | bytes 4456448 | tf_op jit(solution)/shard_map/all_gather | solution.py:148
  78.0 25.0 %copy-start.8 = (bf16[512,64]{0,1:T(8,128)(2,1)}, bf16[512,64]{0,1:T(8,128)(2,1)S(1)}, u32[]{:S(2)}) copy-start(bf16[512,64]{0,1:T(8,128)(2,1)S(1)} %add_convert_fusion) | copy-start | bytes 196612
  92.4 10.8 %copy-start.10 = (s32[384]{0:T(512)S(1)}, s32[384]{0:T(512)}, u32[]{:S(2)}) copy-start(s32[384]{0:T(512)} %param.27) | copy-start | bytes 4612
  94.3 8.8 %all-to-all-start.2 = ((s32[8,2,2]{1,2,0:T(2,128)}), s32[8,2,2]{1,2,0:T(2,128)S(1)}, u32[]{:S(2)}, u32[]{:S(2)}) async-start(s32[8,2,2]{1,2,0:T(2,128)} %copy.96), calls=%async_computation.2 | async-start | bytes 16384 | tf_op jit(solution)/shard_map/all_to_all | solution.py:145
  103.1 40.9 %copy-start.16 = (f32[1024]{0:T(1024)S(1)}, f32[1024]{0:T(1024)}, u32[]{:S(2)}) copy-start(f32[1024]{0:T(1024)} %param.29) | copy-start | bytes 12292
  140.7 3.4 %copy-start.2 = (bf16[2048,1024]{0,1:T(8,128)(2,1)S(1)}, bf16[2048,1024]{0,1:T(8,128)(2,1)}, u32[]{:S(2)}) copy-start(bf16[2048,1024]{0,1:T(8,128)(2,1)} %all-gather.2.cloned.1.call-done) | copy-start | bytes 12582916
  144.1 5.6 %copy-start.5 = (bf16[48,8,8,128]{3,2,1,0:T(8,128)(2,1)S(1)}, bf16[48,8,8,128]{3,2,1,0:T(8,128)(2,1)}, u32[]{:S(2)}) copy-start(bf16[48,8,8,128]{3,2,1,0:T(8,128)(2,1)} %fusion.33) | copy-start | bytes 2359300
  160.7 11.7 %copy-start.13 = (bf16[1024,1024]{1,0:T(8,128)(2,1)S(1)}, bf16[1024,1024]{1,0:T(8,128)(2,1)}, u32[]{:S(2)}) copy-start(bf16[1024,1024]{1,0:T(8,128)(2,1)} %param.32) | copy-start | bytes 6291460
  178.0 12.2 %copy-start.3 = (bf16[1024,1024]{1,0:T(8,128)(2,1)S(1)}, bf16[1024,1024]{1,0:T(8,128)(2,1)}, u32[]{:S(2)}) copy-start(bf16[1024,1024]{1,0:T(8,128)(2,1)} %param.33) | copy-start | bytes 6291460
  178.1 35.2 %copy-start.1 = (bf16[1024,1024]{1,0:T(8,128)(2,1)S(1)}, bf16[1024,1024]{1,0:T(8,128)(2,1)}, u32[]{:S(2)}) copy-start(bf16[1024,1024]{1,0:T(8,128)(2,1)} %param.31) | copy-start | bytes 6291460
  192.1 19.6 %all-to-all-start.3 = ((bf16[16,24,1024]{2,1,0:T(8,128)(2,1)}), bf16[16,24,1024]{2,1,0:T(8,128)(2,1)S(1)}, u32[]{:S(2)}, u32[]{:S(2)}) async-start(bf16[16,24,1024]{2,1,0:T(8,128)(2,1)} %bitcast.18), calls=%async_computation.3 | async-start | bytes 1572864 | tf_op jit(solution)/shard_map/all_to_all | solution.py:25
Sparse Core Ops, SparseCore 0:
  93.4 47.2 all-gather.1
where the time goes:
time: 221 us; the launch traced here: 220 us
  waiting for transfers between devices  79.8 us (36%)
  matrix products  57.7 us (26%)
  other arithmetic  27 us (12%)
  starting transfers between devices  16 us (7%)
  between operations  14.4 us (7%)
  blocking collectives  12.7 us (6%)
  local copies, waits for them, and re-layouts  12.6 us (6%)
    all_gather x1, waiting for transfers between devices, body(): lax.all_gather(flat, 'tensor', axis=1, tiled=True).astype(jnp.float32)  33.9 us
    all_to_all x1, waiting for transfers between devices, sent_and_summed(): lax.all_to_all(blocks, axis, split_axis=0, concat_axis=0, tiled=True)  31.5 us
    dot_general x2, matrix products, attend(): jnp.einsum('hqk,khd->qhd', weights, value_heads, preferred_element_type=j...  14.7 us
    all_to_all x1, waiting for transfers between devices, summed_on_arrival(): lax.all_to_all(blocks, axis, split_axis=0, concat_axis=0, tiled=True)  14.3 us
    dot_general x2, matrix products, attend(): jnp.einsum('qhd,khd->hqk', query_heads, key_heads, preferred_element_type...  14.1 us
    reduce_sum x2, other arithmetic, attend(): total = jnp.sum(expo, axis=2)  13.4 us
    all_to_all x1, blocking collectives, body(): lax.all_to_all(placed.reshape(groups, slots, BLOCK, features), 'dp', spli...  12.7 us
    all_to_all x1, starting transfers between devices, sent_and_summed(): lax.all_to_all(blocks, axis, split_axis=0, concat_axis=0, tiled=True)  7.19 us
  transfers between devices with their start and end apart: 4, of which 3 were waited for; matrix products, arithmetic and copies ran while one was open for 5% of the time, Pallas kernels for 0%

commit v1 on v0

--- a/solution.py
+++ b/solution.py
@@ -145,7 +145,12 @@
     meta = lax.all_to_all(send_meta, "dp", split_axis=0, concat_axis=0, tiled=True)
     flat = slice_grid.reshape(-1, slice_width)
     inner = cross_key.shape[1]
-    values32 = lax.all_gather(flat, "tensor", axis=1, tiled=True).astype(jnp.float32)
+
+    def cut_field_on_mesh(array_in, axis_key):
+        t_next = jnp.concatenate(lax.all_gather(array_in, axis_key), 1)
+        return t_next
+
+    values32 = cut_field_on_mesh(flat, "tensor").astype(jnp.float32)
     scaled = (values32 * final_gain[None, :]).astype(jnp.bfloat16)
     key_sum = jnp.dot(scaled, cross_key, preferred_element_type=jnp.float32)
     value_sum = jnp.dot(scaled, cross_value, preferred_element_type=jnp.float32)

time: 221 us -> 220 us (level)
  no operation moved by 1% of the time
where the time goes in v1:
time: 220 us
  waiting for transfers between devices  79.8 us (36%)
  matrix products  56.5 us (26%)
  other arithmetic  27.6 us (13%)
  starting transfers between devices  16 us (7%)
  between operations  14.4 us (7%)
  local copies, waits for them, and re-layouts  12.7 us (6%)
  blocking collectives  12.7 us (6%)
    all_gather x1, waiting for transfers between devices, cut_field_on_mesh(): t_next = jnp.concatenate(lax.all_gather(array_in, axis_key), 1)  33.9 us
    all_to_all x1, waiting for transfers between devices, sent_and_summed(): lax.all_to_all(blocks, axis, split_axis=0, concat_axis=0, tiled=True)  31.5 us
    dot_general x2, matrix products, attend(): jnp.einsum('hqk,khd->qhd', weights, value_heads, preferred_element_type=j...  14.6 us
    all_to_all x1, waiting for transfers between devices, summed_on_arrival(): lax.all_to_all(blocks, axis, split_axis=0, concat_axis=0, tiled=True)  14.3 us
    dot_general x2, matrix products, attend(): jnp.einsum('qhd,khd->hqk', query_heads, key_heads, preferred_element_type...  14.1 us
    reduce_sum x2, other arithmetic, attend(): total = jnp.sum(expo, axis=2)  13.3 us
    all_to_all x1, blocking collectives, body(): lax.all_to_all(placed.reshape(groups, slots, BLOCK, features), 'dp', spli...  12.7 us
    all_to_all x1, starting transfers between devices, sent_and_summed(): lax.all_to_all(blocks, axis, split_axis=0, concat_axis=0, tiled=True)  7.19 us
  transfers between devices with their start and end apart: 4, of which 3 were waited for; matrix products, arithmetic and copies ran while one was open for 5% of the time, Pallas kernels for 0%

profile of v1, /device:TPU:0, one launch (start us, length us, event | category | flops | bytes accessed | tf_op | source)
XLA Modules:
  0.0 219.6 jit_solution(4871414322046743705)
XLA Ops:
  7.2 1.0 convert_reduce_fusion.2
  8.9 0.9 select_reduce_fusion.2
  10.1 1.5 fusion.16
  11.6 4.4 %fusion.28 = bf16[64,8,8,128]{3,2,1,0:T(8,128)(2,1)} fusion(bf16[1024,1024]{1,0:T(8,128)(2,1)} %param.22, bf16[512,1024]{1,0:T(8,128)(2,1)} %param.17, f32[1024]{0:T(1024)} %param.21, f32[512]{0:T(512)S(1)} %add_rsqrt_fusion.2), kind=kOutput, calls=%fused_computation.45 | convolution fusion | flops 1076363264 | bytes 4200448 | tf_op jit(solution)/shard_map/dot_general | solution.py:95
  16.0 2.3 %fusion.29 = bf16[64,8,8,128]{3,2,1,0:T(8,128)(2,1)} fusion(bf16[1024,1024]{1,0:T(8,128)(2,1)S(1)} %copy-done.12, bf16[512,1024]{1,0:T(8,128)(2,1)S(1)} %copy-done.6, f32[1024]{0:T(1024)S(1)} %copy-done.15, f32[512]{0:T(512)S(1)} %add_rsqrt_fusion.2), kind=kOutput, calls=%fused_computation.46 | convolution fusion | flops 1076363264 | bytes 4200448 | tf_op jit(solution)/shard_map/dot_general | solution.py:98
  18.3 2.3 %convolution_convert_fusion.3 = bf16[512,1024]{1,0:T(8,128)(2,1)} fusion(bf16[1024,1024]{1,0:T(8,128)(2,1)S(1)} %copy-done.13, bf16[512,1024]{1,0:T(8,128)(2,1)S(1)} %copy-done.6, f32[1024]{0:T(1024)S(1)} %copy-done.15, f32[512]{0:T(512)S(1)} %add_rsqrt_fusion.2), kind=kOutput, calls=%fused_computation.42 | convolution fusion | flops 1076363264 | bytes 4200448 | tf_op jit(solution)/shard_map/dot_general | solution.py:99
  20.6 2.3 %copy.108 = bf16[512,1024]{0,1:T(8,128)(2,1)} copy(bf16[512,1024]{1,0:T(8,128)(2,1)} %convolution_convert_fusion.3) | data formatting | bytes 2097152 | tf_op jit(solution)/shard_map/while/body/eval_jaxpr/reshape | solution.py:44
  22.9 4.0 %copy.92 = bf16[1024,1024]{0,1:T(8,128)(2,1)} copy(bf16[1024,1024]{1,0:T(8,128)(2,1)} %param.25) | data formatting | bytes 4194304 | tf_op args[8]
  27.1 3.2 %fusion.7 = (f32[8,512]{1,0:T(8,128)S(1)}, f32[8,512,512]{1,2,0:T(8,128)S(1)}) fusion(pred[512,512]{0,1:T(8,128)(4,1)S(1)} %compare_and_fusion, bf16[64,8,8,128]{3,2,1,0:T(8,128)(2,1)} %fusion.29, bf16[64,8,8,128]{3,2,1,0:T(8,128)(2,1)} %fusion.28), kind=kOutput, calls=%fused_computation.15 | convolution fusion | flops 543158272 | bytes 10764288 | tf_op jit(solution)/shard_map/while/body/eval_jaxpr/qhd,khd->hqk/dot_general | solution.py:45
  30.3 1.7 fusion.8
  32.1 2.6 %fusion.19 = bf16[512,8,128]{0,2,1:T(8,128)(2,1)S(1)} fusion(bf16[512,8,128]{0,2,1:T(8,128)(2,1)S(1)} %bitcast.78, f32[8,512,512]{1,2,0:T(8,128)S(1)} %get-tuple-element.33, f32[8,512]{1,0:T(8,128)S(1)} %get-tuple-element.32, pred[512,512]{0,1:T(8,128)(4,1)S(1)} %compare_and_fusion, f32[512,8]{0,1:T(8,128)S(1)} %bitcast.80), kind=kOutput, calls=%fused_computation.30 | convolution fusion | flops 546308096 | bytes 10780672 | tf_op jit(solution)/shard_map/while/body/eval_jaxpr/hqk,khd->qhd/dot_general | solution.py:53
  34.7 2.5 %convolution_bitcast_fusion = f32[16,512,64]{1,2,0:T(8,128)} fusion(bf16[512,1024,1]{0,1,2:T(8,128)(2,1)S(1)} %bitcast.85, bf16[16,64,1024]{2,1,0:T(8,128)(2,1)S(1)} %bitcast.77), kind=kOutput, calls=%fused_computation.33 | convolution fusion | flops 1073741824 | bytes 5242880 | tf_op jit(solution)/shard_map/dot_general | solution.py:116
  37.2 7.2 %all-to-all-start = ((f32[16,512,64]{1,2,0:T(8,128)}), f32[16,512,64]{1,2,0:T(8,128)}, u32[]{:S(2)}, u32[]{:S(2)}) async-start(f32[16,512,64]{1,2,0:T(8,128)} %convolution_bitcast_fusion), calls=%async_computation | async-start | bytes 4194304 | tf_op jit(solution)/shard_map/all_to_all | solution.py:19
  44.7 31.5 %all-to-all-done = f32[16,512,64]{1,2,0:T(8,128)} async-done(((f32[16,512,64]{1,2,0:T(8,128)}), f32[16,512,64]{1,2,0:T(8,128)}, u32[]{:S(2)}, u32[]{:S(2)}) %all-to-all-start) | async-done | bytes 2097184 | tf_op jit(solution)/shard_map/all_to_all | solution.py:19
  76.2 1.8 reduce_sum.122
  79.4 12.7 %all_to_all.20 = bf16[8,2,128,64]{2,3,1,0:T(8,128)(2,1)S(1)} all-to-all(bf16[8,2,128,64]{2,3,1,0:T(8,128)(2,1)S(1)} %copy.95), channel_id=1, replica_groups=mesh['dp'=8,'tensor'=16] {'dp'}, dimensions={0} | all-to-all | bytes 524288 | tf_op jit(solution)/shard_map/all_to_all | solution.py:138
  94.3 3.5 %all-to-all-start.2 = ((s32[8,2,2]{1,2,0:T(2,128)}), s32[8,2,2]{1,2,0:T(2,128)S(1)}, u32[]{:S(2)}, u32[]{:S(2)}) async-start(s32[8,2,2]{1,2,0:T(2,128)} %copy.97), calls=%async_computation.2 | async-start | bytes 16384 | tf_op jit(solution)/shard_map/all_to_all | solution.py:145
  97.8 1.4 fusion.22
  99.2 3.9 %fusion.30 = bf16[48,8,8,128]{3,2,1,0:T(8,128)(2,1)} fusion(bf16[1024,1024]{1,0:T(8,128)(2,1)} %param.30, bf16[384,1024]{1,0:T(8,128)(2,1)} %param.26, f32[1024]{0:T(1024)S(1)} %copy-done.16, f32[384]{0:T(512)S(1)} %add_rsqrt_fusion.1), kind=kOutput, calls=%fused_computation.47 | convolution fusion | flops 807272448 | bytes 3675648 | tf_op jit(solution)/shard_map/dot_general | solution.py:170
  103.3 1.3 bitcast_and_fusion
  104.6 2.2 copy.102
  106.8 33.9 %all-gather.2.cloned.1.call-done = bf16[16,2048,64]{1,2,0:T(8,128)(2,1)} async-done(((bf16[1,2048,64]{1,2,0:T(8,128)(2,1)}), bf16[16,2048,64]{1,2,0:T(8,128)(2,1)}) %all-gather.2.cloned.1.call-update) | async-done | bytes 4194320 | tf_op jit(solution)/shard_map/all_gather | solution.py:150
  140.7 3.2 %multiply_reduce_fusion = f32[2048]{0:T(1024)S(1)} fusion(bf16[16,2048,64]{1,2,0:T(8,128)(2,1)} %all-gather.2.cloned.1.call-done), kind=kLoop, calls=%fused_computation.12 | loop fusion | flops 6289408 | bytes 4202496 | tf_op jit(solution)/shard_map/reduce_sum | solution.py:157
  144.9 5.1 %multiply_convert_fusion = bf16[2048,1024]{0,1:T(8,128)(2,1)S(1)} fusion(bf16[2048,1024]{0,1:T(8,128)(2,1)S(1)} %fusion.6, bf16[1024,1024]{1,0:T(8,128)(2,1)S(1)} %copy-done, f32[2048]{0:T(1024)S(1)} %add_rsqrt_fusion), kind=kOutput, calls=%fused_computation.10 | convolution fusion | flops 4299161600 | bytes 10493952 | tf_op jit(solution)/shard_map/dot_general | solution.py:155
  150.0 5.1 %multiply_convert_fusion.1 = bf16[2048,1024]{0,1:T(8,128)(2,1)S(1)} fusion(bf16[2048,1024]{0,1:T(8,128)(2,1)S(1)} %fusion.6, bf16[1024,1024]{1,0:T(8,128)(2,1)S(1)} %copy-done.14, f32[2048]{0:T(1024)S(1)} %add_rsqrt_fusion), kind=kOutput, calls=%fused_computation.11 | convolution fusion | flops 4299161600 | bytes 10493952 | tf_op jit(solution)/shard_map/dot_general | solution.py:156
  155.1 10.9 %fusion = (f32[8,384]{1,0:T(8,128)S(1)}, f32[8,384,2048]{2,1,0:T(8,128)}) fusion(pred[384,2048]{1,0:T(8,128)(4,1)S(1)} %copy.102, bf16[2048,8,128]{0,2,1:T(8,128)(2,1)S(1)} %bitcast.76, bf16[48,8,8,128]{3,2,1,0:T(8,128)(2,1)S(1)} %copy-done.5), kind=kOutput, calls=%fused_computation.2 | convolution fusion | flops 1629484032 | bytes 30945280 | tf_op jit(solution)/shard_map/qhd,khd->hqk/dot_general | solution.py:45
  166.0 11.6 %fusion.1 = f32[8,384]{1,0:T(8,128)S(1)} fusion(f32[8,384,2048]{2,1,0:T(8,128)} %get-tuple-element.35, f32[8,384]{1,0:T(8,128)S(1)} %get-tuple-element.34, pred[384,2048]{1,0:T(8,128)(4,1)S(1)} %copy.102), kind=kLoop, calls=%fused_computation.3 | loop fusion | flops 25162752 | bytes 25976832 | tf_op jit(solution)/shard_map/reduce_sum | solution.py:51
  177.6 12.0 %fusion.25 = bf16[384,8,128]{0,2,1:T(8,128)(2,1)S(1)} fusion(bf16[2048,8,128]{0,2,1:T(8,128)(2,1)S(1)} %bitcast.84, f32[8,384,2048]{2,1,0:T(8,128)} %get-tuple-element.35, f32[8,384]{1,0:T(8,128)S(1)} %get-tuple-element.34, pred[384,2048]{1,0:T(8,128)(4,1)S(1)} %copy.102, f32[384,8]{0,1:T(8,128)S(1)} %bitcast.83), kind=kOutput, calls=%fused_computation.38 | convolution fusion | flops 1636564992 | bytes 30957568 | tf_op jit(solution)/shard_map/hqk,khd->qhd/dot_general | solution.py:53
  189.7 1.9 convolution_convert_fusion.4
  191.5 5.3 %all-to-all-start.3 = ((bf16[16,24,1024]{2,1,0:T(8,128)(2,1)}), bf16[16,24,1024]{2,1,0:T(8,128)(2,1)S(1)}, u32[]{:S(2)}, u32[]{:S(2)}) async-start(bf16[16,24,1024]{2,1,0:T(8,128)(2,1)} %bitcast.20), calls=%async_computation.3 | async-start | bytes 1572864 | tf_op jit(solution)/shard_map/all_to_all | solution.py:25
  196.8 14.3 %all-to-all-done.3 = bf16[16,24,1024]{2,1,0:T(8,128)(2,1)S(1)} async-done(((bf16[16,24,1024]{2,1,0:T(8,128)(2,1)}), bf16[16,24,1024]{2,1,0:T(8,128)(2,1)S(1)}, u32[]{:S(2)}, u32[]{:S(2)}) %all-to-all-start.3) | async-done | bytes 786464 | tf_op jit(solution)/shard_map/all_to_all | solution.py:25
  211.3 1.4 add_convert_fusion.1
  (68 shorter events, 6.4 us)
Async XLA Ops:
  7.2 137.7 %copy-start = (bf16[1024,1024]{1,0:T(8,128)(2,1)S(1)}, bf16[1024,1024]{1,0:T(8,128)(2,1)}, u32[]{:S(2)}) copy-start(bf16[1024,1024]{1,0:T(8,128)(2,1)} %param.31) | copy-start | bytes 6291460
  11.6 4.4 %copy-start.6 = (bf16[512,1024]{1,0:T(8,128)(2,1)S(1)}, bf16[512,1024]{1,0:T(8,128)(2,1)}, u32[]{:S(2)}) copy-start(bf16[512,1024]{1,0:T(8,128)(2,1)} %param.17) | copy-start | bytes 3145732
  11.6 4.4 %copy-start.12 = (bf16[1024,1024]{1,0:T(8,128)(2,1)S(1)}, bf16[1024,1024]{1,0:T(8,128)(2,1)}, u32[]{:S(2)}) copy-start(bf16[1024,1024]{1,0:T(8,128)(2,1)} %param.23) | copy-start | bytes 6291460
  11.6 4.4 %copy-start.15 = (f32[1024]{0:T(1024)S(1)}, f32[1024]{0:T(1024)}, u32[]{:S(2)}) copy-start(f32[1024]{0:T(1024)} %param.21) | copy-start | bytes 12292
  16.0 2.3 %copy-start.13 = (bf16[1024,1024]{1,0:T(8,128)(2,1)S(1)}, bf16[1024,1024]{1,0:T(8,128)(2,1)}, u32[]{:S(2)}) copy-start(bf16[1024,1024]{1,0:T(8,128)(2,1)} %param.24) | copy-start | bytes 6291460
  30.3 1.8 copy-start.7
  32.1 2.6 %copy-start.4 = (bf16[1024,1024]{0,1:T(8,128)(2,1)S(1)}, bf16[1024,1024]{0,1:T(8,128)(2,1)}, u32[]{:S(2)}) copy-start(bf16[1024,1024]{0,1:T(8,128)(2,1)} %copy.92) | copy-start | bytes 6291460
  37.2 39.0 %all-to-all-start = ((f32[16,512,64]{1,2,0:T(8,128)}), f32[16,512,64]{1,2,0:T(8,128)}, u32[]{:S(2)}, u32[]{:S(2)}) async-start(f32[16,512,64]{1,2,0:T(8,128)} %convolution_bitcast_fusion), calls=%async_computation | async-start | bytes 4194304 | tf_op jit(solution)/shard_map/all_to_all | solution.py:19
  44.4 49.0 %copy-start.9 = (s32[4]{0:T(128)S(1)}, s32[4]{0:T(128)}, u32[]{:S(2)}) copy-start(s32[4]{0:T(128)} %param.18) | copy-start | bytes 52
  44.4 54.8 %copy-start.16 = (f32[1024]{0:T(1024)S(1)}, f32[1024]{0:T(1024)}, u32[]{:S(2)}) copy-start(f32[1024]{0:T(1024)} %param.28) | copy-start | bytes 12292
  44.4 96.2 %all-gather.2.cloned.1.call-start = ((), (), s32[]{:S(2)}) async-start(), calls=%async_computation.4 | async-start | bytes 4456448 | tf_op jit(solution)/shard_map/all_gather | solution.py:150
  78.0 25.0 %copy-start.8 = (bf16[512,64]{0,1:T(8,128)(2,1)}, bf16[512,64]{0,1:T(8,128)(2,1)S(1)}, u32[]{:S(2)}) copy-start(bf16[512,64]{0,1:T(8,128)(2,1)S(1)} %add_convert_fusion) | copy-start | bytes 196612
  92.4 10.8 %copy-start.11 = (s32[384]{0:T(512)S(1)}, s32[384]{0:T(512)}, u32[]{:S(2)}) copy-start(s32[384]{0:T(512)} %param.27) | copy-start | bytes 4612
  94.3 8.8 %all-to-all-start.2 = ((s32[8,2,2]{1,2,0:T(2,128)}), s32[8,2,2]{1,2,0:T(2,128)S(1)}, u32[]{:S(2)}, u32[]{:S(2)}) async-start(s32[8,2,2]{1,2,0:T(2,128)} %copy.97), calls=%async_computation.2 | async-start | bytes 16384 | tf_op jit(solution)/shard_map/all_to_all | solution.py:145
  103.1 40.8 %copy-start.10 = (f32[1024]{0:T(1024)S(1)}, f32[1024]{0:T(1024)}, u32[]{:S(2)}) copy-start(f32[1024]{0:T(1024)} %param.29) | copy-start | bytes 12292
  140.7 3.4 %copy-start.2 = (bf16[16,2048,64]{1,2,0:T(8,128)(2,1)S(1)}, bf16[16,2048,64]{1,2,0:T(8,128)(2,1)}, u32[]{:S(2)}) copy-start(bf16[16,2048,64]{1,2,0:T(8,128)(2,1)} %all-gather.2.cloned.1.call-done) | copy-start | bytes 12582916
  144.9 5.1 %copy-start.14 = (bf16[1024,1024]{1,0:T(8,128)(2,1)S(1)}, bf16[1024,1024]{1,0:T(8,128)(2,1)}, u32[]{:S(2)}) copy-start(bf16[1024,1024]{1,0:T(8,128)(2,1)} %param.32) | copy-start | bytes 6291460
  150.0 5.1 %copy-start.5 = (bf16[48,8,8,128]{3,2,1,0:T(8,128)(2,1)S(1)}, bf16[48,8,8,128]{3,2,1,0:T(8,128)(2,1)}, u32[]{:S(2)}) copy-start(bf16[48,8,8,128]{3,2,1,0:T(8,128)(2,1)} %fusion.30) | copy-start | bytes 2359300
  177.6 12.1 %copy-start.3 = (bf16[1024,1024]{1,0:T(8,128)(2,1)S(1)}, bf16[1024,1024]{1,0:T(8,128)(2,1)}, u32[]{:S(2)}) copy-start(bf16[1024,1024]{1,0:T(8,128)(2,1)} %param.33) | copy-start | bytes 6291460
  177.6 35.1 %copy-start.1 = (bf16[1024,1024]{1,0:T(8,128)(2,1)S(1)}, bf16[1024,1024]{1,0:T(8,128)(2,1)}, u32[]{:S(2)}) copy-start(bf16[1024,1024]{1,0:T(8,128)(2,1)} %param.31) | copy-start | bytes 6291460
  191.5 19.6 %all-to-all-start.3 = ((bf16[16,24,1024]{2,1,0:T(8,128)(2,1)}), bf16[16,24,1024]{2,1,0:T(8,128)(2,1)S(1)}, u32[]{:S(2)}, u32[]{:S(2)}) async-start(bf16[16,24,1024]{2,1,0:T(8,128)(2,1)} %bitcast.20), calls=%async_computation.3 | async-start | bytes 1572864 | tf_op jit(solution)/shard_map/all_to_all | solution.py:25
Sparse Core Ops, SparseCore 0:
  93.4 47.2 all-gather.1
